TPU v7x, 32 devices: a whole 2x2x4 slice. The times are simulated.
32 devices in a mesh: leaf: 2 (over core), row: 4 (over y, x), col: 4 (over z).
Axes of the slice: x: 2, y: 2, z: 4, core: 2. Of those that a mesh axis runs over, the one named last changes fastest.
Arguments:
- sketch_leaf: bfloat16 [16384, 256], P(('leaf', 'row'), 'col'), may hold values from -6 to 6
- sketch_sep: bfloat16 [8192, 256], P(('row', 'col')), may hold values from -6 to 6
- leaf_inverse: bfloat16 [16384, 8192], P(('leaf', 'col'), 'row'), as said below
- coupling: bfloat16 [16384, 2048], P(('leaf', 'col'), 'row'), may hold values from -0.0625 to 0.0625
- sep_inverse: bfloat16 [8192, 8192], P('leaf', ('row', 'col'))
- front_map: int32 [2, 16], replicated, may hold values from 0 to 63, as said below
Outputs:
- sketch_out_leaf: float32 [16384, 256], P(('leaf', 'row'), 'col')
- sketch_out_sep: float32 [8192, 256], P(('row', 'col'))
Inputs may be any that keep to these rules, and one draw needn't show every extreme that they name: `front_map`: row block q of every section's coupling lies in separator blocks q * 4 to q * 4 + 3. leaf_inverse and sep_inverse are inverses of lower triangular factor blocks (in natural order), stored in block-cyclic order.
All inputs are finite; a program needn't handle non-finite values.
Results may differ from a plain program's by a relative error of at most 0.024.
Values may be sent and summed in bfloat16 or wider, within the bound.
No kernel may reach another device: no remote copies, remote signals or barrier semaphores. Data moves between devices by JAX's collectives and lax.ppermute only.
A program may use at most 64 MiB of HBM per device.

v0:
```python
import jax
import jax.numpy as jnp
from jax import lax
from jax.sharding import PartitionSpec as P


def contract_rows(left, right):
    return lax.dot_general(
        left, right, (((0,), (0,)), ((), ())), preferred_element_type=jnp.float32
    )


def shards(sketch_leaf, sketch_sep, leaf_inverse, coupling, sep_inverse, front_map):
    columns = sketch_leaf.shape[1] * lax.axis_size("col")
    q_index = lax.axis_index("row") * lax.axis_size("col") + lax.axis_index("col")
    section = lax.axis_index("leaf")
    partial_value = jnp.dot(
        leaf_inverse,
        lax.all_gather(sketch_leaf, "col", axis=1, tiled=True),
        preferred_element_type=jnp.float32,
    )
    front_z = lax.psum_scatter(partial_value, "row", scatter_dimension=1, tiled=True).astype(
        jnp.bfloat16
    )
    coupled_part = contract_rows(coupling, lax.all_gather(front_z, "row", axis=1, tiled=True))
    coupled = lax.psum_scatter(coupled_part, "col", scatter_dimension=0, tiled=True).astype(
        jnp.bfloat16
    )
    block_rows = coupled.shape[0]
    group = sketch_sep.shape[0] // block_rows
    own_slot = front_map[section, q_index] - q_index * group
    blocks = lax.all_gather(coupled, "leaf", axis=0, tiled=True)
    slots = front_map[:, q_index] - q_index * group
    place = (slots[:, None] == jnp.arange(group, dtype=jnp.int32)[None, :]).astype(jnp.bfloat16)
    stacked = blocks.reshape(slots.shape[0], block_rows, columns)
    total = jnp.einsum("sg,sik->gik", place, stacked, preferred_element_type=jnp.float32).reshape(
        group * block_rows, columns
    )
    sep_rhs = (sketch_sep.astype(jnp.float32) - total).astype(jnp.bfloat16)
    sep_part = jnp.dot(sep_inverse, sep_rhs, preferred_element_type=jnp.float32)
    sep_mid = lax.psum(sep_part.astype(jnp.bfloat16), ("row", "col"))
    sketch_out_sep = lax.psum(
        contract_rows(sep_inverse, sep_mid).astype(jnp.bfloat16), "leaf"
    ).astype(jnp.float32)
    sep_round = sketch_out_sep.astype(jnp.bfloat16)
    pulled = lax.dynamic_slice_in_dim(sep_round, own_slot * block_rows, block_rows, 0)
    back_part = jnp.dot(
        coupling,
        lax.all_gather(pulled, "col", axis=0, tiled=True),
        preferred_element_type=jnp.float32,
    )
    back_slice = lax.psum_scatter(
        back_part.astype(jnp.bfloat16), "row", scatter_dimension=1, tiled=True
    ).astype(jnp.float32)
    leaf_rhs = (front_z.astype(jnp.float32) - back_slice).astype(jnp.bfloat16)
    out_part = contract_rows(leaf_inverse, lax.all_gather(leaf_rhs, "row", axis=1, tiled=True))
    sketch_out_leaf = lax.psum_scatter(
        out_part.astype(jnp.bfloat16), "col", scatter_dimension=1, tiled=True
    ).astype(jnp.float32)
    return (sketch_out_leaf, sketch_out_sep)


def solution(mesh):
    placed = (
        P(("leaf", "row"), "col"),
        P(("row", "col"), None),
        P(("leaf", "col"), "row"),
        P(("leaf", "col"), "row"),
        P("leaf", ("row", "col")),
        P(),
    )
    return jax.shard_map(
        shards,
        mesh=mesh,
        in_specs=placed,
        out_specs=(P(("leaf", "row"), "col"), P(("row", "col"), None)),
        check_vma=False,
    )
```

profile of v0, /device:TPU:0, one launch (start us, length us, event | category | flops | bytes accessed | tf_op | source)
XLA Modules:
  0.0 407.7 jit_solution(16510389504449765819)
XLA Ops:
  7.2 0.7 all-gather.4.cloned.1.call-update
  8.0 32.3 %all-gather.4.cloned.1.call-done = bf16[2048,256]{0,1:T(8,128)(2,1)} async-done(((bf16[2048,64]{0,1:T(8,128)(2,1)}), bf16[2048,256]{0,1:T(8,128)(2,1)}) %all-gather.4.cloned.1.call-update) | async-done | bytes 1048592 | tf_op jit(solution)/shard_map/all_gather | solution.py:19
  40.3 7.3 %fusion.10 = f32[2048,256]{0,1:T(8,128)} fusion(bf16[2048,2048]{1,0:T(8,128)(2,1)} %param.8, bf16[2048,256]{0,1:T(8,128)(2,1)} %all-gather.4.cloned.1.call-done), kind=kOutput, calls=%fused_computation.19 | convolution fusion | flops 2147483648 | bytes 11534336 | tf_op jit(solution)/shard_map/dot_general | solution.py:17
  47.7 34.7 %reduce-scatter.5.cloned.1.call-done = f32[2048,64]{0,1:T(8,128)} async-done(((f32[2048,256]{0,1:T(8,128)}), f32[2048,64]{0,1:T(8,128)}) %reduce-scatter.5.cloned.1.call-update) | async-done | bytes 524304 | tf_op jit(solution)/shard_map/reduce_scatter | solution.py:22
  82.3 1.8 convert_element_type.53
  84.2 27.1 %all-gather.6.cloned.1.call-done = bf16[2048,256]{0,1:T(8,128)(2,1)} async-done(((bf16[2048,64]{0,1:T(8,128)(2,1)}), bf16[2048,256]{0,1:T(8,128)(2,1)}) %all-gather.6.cloned.1.call-update) | async-done | bytes 1048592 | tf_op jit(solution)/shard_map/all_gather | solution.py:25
  111.3 2.7 convolution_bitcast_fusion
  114.1 0.2 subtract_reduce_fusion
  114.3 21.7 %reduce-scatter.7.cloned.1.call-done = f32[128,256]{0,1:T(8,128)} async-done(((f32[512,256]{0,1:T(8,128)}), f32[128,256]{0,1:T(8,128)}) %reduce-scatter.7.cloned.1.call-update) | async-done | bytes 131088 | tf_op jit(solution)/shard_map/reduce_scatter | solution.py:26
  136.0 0.9 convert_element_type.56
  136.9 1.9 all_gather.17
  138.9 0.1 copy.10
  139.0 0.4 fusion.5
  139.5 0.1 copy.11
  139.6 0.1 fusion.4
  139.7 4.8 %fusion = bf16[4096,256]{0,1:T(8,128)(2,1)} fusion(bf16[512,256]{1,0:T(8,128)(2,1)S(1)} %fusion.4, bf16[4096,512]{1,0:T(8,128)(2,1)} %param.10), kind=kOutput, calls=%fused_computation.1 | convolution fusion | flops 1074790400 | bytes 6553600 | tf_op jit(solution)/shard_map/dot_general | solution.py:40
  144.5 125.0 %all-reduce.3.cloned.1.call-done = bf16[4096,256]{0,1:T(8,128)(2,1)} async-done(((bf16[4096,256]{0,1:T(8,128)(2,1)}), bf16[4096,256]{0,1:T(8,128)(2,1)}) %all-reduce.3.cloned.1.call-update) | async-done | bytes 2097168 | tf_op jit(solution)/shard_map/psum | solution.py:41
  269.5 4.8 %fusion.3 = bf16[512,256]{0,1:T(8,128)(2,1)} fusion(bf16[4096,256]{0,1:T(8,128)(2,1)} %all-reduce.3.cloned.1.call-done, bf16[4096,512]{1,0:T(8,128)(2,1)} %param.10), kind=kOutput, calls=%fused_computation.8 | convolution fusion | flops 1073872896 | bytes 6553600 | tf_op jit(solution)/shard_map/dot_general | solution.py:8
  274.3 0.0 reduce-scatter.9.cloned.1.call-start
  274.4 0.6 dynamic_slice.10
  275.6 16.3 %all-reduce.5.cloned.1.call-done = bf16[512,256]{0,1:T(8,128)(2,1)} async-done(((bf16[512,256]{0,1:T(8,128)(2,1)}), bf16[512,256]{0,1:T(8,128)(2,1)}) %all-reduce.5.cloned.1.call-update) | async-done | bytes 262160 | tf_op jit(solution)/shard_map/psum | solution.py:42
  291.9 0.8 constant_dynamic-slice_fusion
  292.8 13.1 %all_gather.18 = bf16[512,256]{0,1:T(8,128)(2,1)S(1)} all-gather(bf16[128,256]{0,1:T(8,128)(2,1)S(1)} %constant_dynamic-slice_fusion), channel_id=1, replica_groups=mesh['leaf'=2,'row'=4,'col'=4] {'col'}, dimensions={0}, use_global_device_ids=true | all-gather | bytes 327680 | tf_op jit(solution)/shard_map/all_gather | solution.py:49
  305.9 1.7 fusion.2
  307.7 28.2 %reduce-scatter.9.cloned.1.call-done = bf16[2048,64]{0,1:T(8,128)(2,1)} async-done(((bf16[2048,256]{0,1:T(8,128)(2,1)}), bf16[2048,64]{0,1:T(8,128)(2,1)}) %reduce-scatter.9.cloned.1.call-update) | async-done | bytes 262160 | tf_op jit(solution)/shard_map/reduce_scatter | solution.py:52
  335.9 1.7 subtract_convert_fusion
  337.7 0.0 reduce-scatter.11.cloned.1.call-start
  337.7 27.2 %all-gather.8.cloned.1.call-done = bf16[2048,256]{0,1:T(8,128)(2,1)} async-done(((bf16[2048,64]{0,1:T(8,128)(2,1)}), bf16[2048,256]{0,1:T(8,128)(2,1)}) %all-gather.8.cloned.1.call-update) | async-done | bytes 1048592 | tf_op jit(solution)/shard_map/all_gather | solution.py:56
  364.9 7.0 %fusion.1 = bf16[2048,256]{0,1:T(8,128)(2,1)} fusion(bf16[2048,256]{0,1:T(8,128)(2,1)} %all-gather.8.cloned.1.call-done, bf16[2048,2048]{1,0:T(8,128)(2,1)} %param.8), kind=kOutput, calls=%fused_computation.4 | convolution fusion | flops 2148007936 | bytes 10485760 | tf_op jit(solution)/shard_map/dot_general | solution.py:8
  371.9 0.9 copy.12
  372.9 26.5 %reduce-scatter.11.cloned.1.call-done = bf16[2048,64]{0,1:T(8,128)(2,1)} async-done(((bf16[2048,256]{0,1:T(8,128)(2,1)}), bf16[2048,64]{0,1:T(8,128)(2,1)}) %reduce-scatter.11.cloned.1.call-update) | async-done | bytes 262160 | tf_op jit(solution)/shard_map/reduce_scatter | solution.py:57
  399.4 1.8 convert_element_type.68
  (26 shorter events, 0.5 us)
Async XLA Ops:
  7.2 104.1 %copy-start = (bf16[2048,512]{1,0:T(8,128)(2,1)S(1)}, bf16[2048,512]{1,0:T(8,128)(2,1)}, u32[]{:S(2)}) copy-start(bf16[2048,512]{1,0:T(8,128)(2,1)} %param.9) | copy-start | bytes 6291460
  7.2 33.1 %all-gather.4.cloned.1.call-start = ((), (), s32[]{:S(2)}) async-start(), calls=%async_computation.4 | async-start | bytes 1310720 | tf_op jit(solution)/shard_map/all_gather | solution.py:19
  7.9 74.4 %reduce-scatter.5.cloned.1.call-start = ((), (), s32[]{:S(2)}) async-start(), calls=%async_computation.5 | async-start | bytes 2621440 | tf_op jit(solution)/shard_map/reduce_scatter | solution.py:22
  47.6 63.7 %all-gather.6.cloned.1.call-start = ((), (), s32[]{:S(2)}) async-start(), calls=%async_computation.6 | async-start | bytes 1310720 | tf_op jit(solution)/shard_map/all_gather | solution.py:25
  84.1 30.0 %copy-start.4 = (s32[2,16]{1,0:T(2,128)S(1)}, s32[2,16]{1,0:T(2,128)}, u32[]{:S(2)}) copy-start(s32[2,16]{1,0:T(2,128)} %param.11) | copy-start | bytes 388
  84.2 51.9 %reduce-scatter.7.cloned.1.call-start = ((), (), s32[]{:S(2)}) async-start(), calls=%async_computation.7 | async-start | bytes 655360 | tf_op jit(solution)/shard_map/reduce_scatter | solution.py:26
  114.0 25.5 %copy-start.3 = (bf16[512,256]{1,0:T(8,128)(2,1)S(1)}, bf16[512,256]{1,0:T(8,128)(2,1)}, u32[]{:S(2)}) copy-start(bf16[512,256]{1,0:T(8,128)(2,1)} %param.7) | copy-start | bytes 786436
  114.1 155.5 %all-reduce.3.cloned.1.call-start = ((), (), s32[]{:S(2)}) async-start(), calls=%async_computation.8 | async-start | bytes 4194304 | tf_op jit(solution)/shard_map/psum | solution.py:41
  144.5 147.4 %all-reduce.5.cloned.1.call-start = ((), (), s32[]{:S(2)}) async-start(), calls=%async_computation.9 | async-start | bytes 524288 | tf_op jit(solution)/shard_map/psum | solution.py:42
  274.3 61.6 %reduce-scatter.9.cloned.1.call-start = ((), (), s32[]{:S(2)}) async-start(), calls=%async_computation.10 | async-start | bytes 1310720 | tf_op jit(solution)/shard_map/reduce_scatter | solution.py:52
  305.9 30.0 %copy-start.1 = (f32[2048,64]{0,1:T(8,128)S(1)}, f32[2048,64]{0,1:T(8,128)}, u32[]{:S(2)}) copy-start(f32[2048,64]{0,1:T(8,128)} %reduce-scatter.5.cloned.1.call-done) | copy-start | bytes 1572868
  307.7 57.2 %all-gather.8.cloned.1.call-start = ((), (), s32[]{:S(2)}) async-start(), calls=%async_computation.11 | async-start | bytes 1310720 | tf_op jit(solution)/shard_map/all_gather | solution.py:56
  337.6 34.3 %copy-start.2 = (bf16[512,256]{0,1:T(8,128)(2,1)S(1)}, bf16[512,256]{0,1:T(8,128)(2,1)}, u32[]{:S(2)}) copy-start(bf16[512,256]{0,1:T(8,128)(2,1)} %all-reduce.5.cloned.1.call-done) | copy-start | bytes 786436
  337.7 61.7 %reduce-scatter.11.cloned.1.call-start = ((), (), s32[]{:S(2)}) async-start(), calls=%async_computation.12 | async-start | bytes 1310720 | tf_op jit(solution)/shard_map/reduce_scatter | solution.py:57
Sparse Core Ops, SparseCore 0:
  9.6 30.6 all-gather.3
  47.7 34.5 reduce-scatter.4
  84.8 26.4 all-gather.5
  114.2 21.8 reduce-scatter.6
  144.6 124.8 all-reduce.2
  274.4 17.4 all-reduce.4
  307.8 28.0 reduce-scatter.8
  338.3 26.4 all-gather.7
  372.0 27.2 reduce-scatter.10
where the time goes:
time: 408 us
  waiting for transfers between devices  340 us (83%)
  matrix products  28.8 us (7%)
  blocking collectives  15.1 us (4%)
  between operations  14.6 us (4%)
  other arithmetic  6.41 us (2%)
    psum x1, waiting for transfers between devices, shards(): sep_mid = lax.psum(sep_part.astype(jnp.bfloat16), ('row', 'col'))  125 us
    reduce_scatter x1, waiting for transfers between devices, shards(): lax.psum_scatter(partial_value, 'row', scatter_dimension=1, tiled=True)  34.7 us
    all_gather x1, waiting for transfers between devices, shards(): lax.all_gather(sketch_leaf, 'col', axis=1, tiled=True)  32.3 us
    reduce_scatter x1, waiting for transfers between devices, shards(): lax.psum_scatter(back_part.astype(jnp.bfloat16), 'row', scatter_dimension...  28.2 us
    all_gather x1, waiting for transfers between devices, shards(): lax.all_gather(leaf_rhs, 'row', axis=1, tiled=True)  27.2 us
    all_gather x1, waiting for transfers between devices, shards(): lax.all_gather(front_z, 'row', axis=1, tiled=True)  27.1 us
    reduce_scatter x1, waiting for transfers between devices, shards(): lax.psum_scatter(out_part.astype(jnp.bfloat16), 'col', scatter_dimension=...  26.5 us
    reduce_scatter x1, waiting for transfers between devices, shards(): lax.psum_scatter(coupled_part, 'col', scatter_dimension=0, tiled=True)  21.7 us
  transfers between devices with their start and end apart: 9, of which 9 were waited for; matrix products, arithmetic and copies ran while one was open for 0% of the time, Pallas kernels for 0%

commit v1 on v0

--- a/solution.py
+++ b/solution.py
@@ -38,7 +38,8 @@
     )
     sep_rhs = (sketch_sep.astype(jnp.float32) - total).astype(jnp.bfloat16)
     sep_part = jnp.dot(sep_inverse, sep_rhs, preferred_element_type=jnp.float32)
-    sep_mid = lax.psum(sep_part.astype(jnp.bfloat16), ("row", "col"))
+    inner = lax.psum(sep_part.astype(jnp.bfloat16), "col")
+    sep_mid = lax.psum(inner, "row")
     sketch_out_sep = lax.psum(
         contract_rows(sep_inverse, sep_mid).astype(jnp.bfloat16), "leaf"
     ).astype(jnp.float32)

time: 408 us -> 440 us (1.078)
  waiting for transfers between devices: 340 us -> 372 us
    psum x1 -> x2, waiting for transfers between devices: 125 us -> 156 us  [the longest x1 84.5 us: shards(): inner = lax.psum(sep_part.astype(jnp.bfloat16), 'col')]
  transfers between devices with their start and end apart: 9 -> 10, of which waited for: 9 -> 10; matrix products, arithmetic and copies ran while one was open for 0% -> 0% of each run, Pallas kernels for 0% -> 0%
where the time goes in v1:
time: 440 us
  waiting for transfers between devices  372 us (85%)
  matrix products  28.8 us (7%)
  blocking collectives  15.1 us (3%)
  between operations  14.9 us (3%)
  other arithmetic  6.41 us (1%)
    psum x1, waiting for transfers between devices, shards(): inner = lax.psum(sep_part.astype(jnp.bfloat16), 'col')  84.5 us
    psum x1, waiting for transfers between devices, shards(): sep_mid = lax.psum(inner, 'row')  71.4 us
    reduce_scatter x1, waiting for transfers between devices, shards(): lax.psum_scatter(partial_value, 'row', scatter_dimension=1, tiled=True)  34.7 us
    all_gather x1, waiting for transfers between devices, shards(): lax.all_gather(sketch_leaf, 'col', axis=1, tiled=True)  32.3 us
    reduce_scatter x1, waiting for transfers between devices, shards(): lax.psum_scatter(back_part.astype(jnp.bfloat16), 'row', scatter_dimension...  28.2 us
    all_gather x1, waiting for transfers between devices, shards(): lax.all_gather(leaf_rhs, 'row', axis=1, tiled=True)  27.2 us
    all_gather x1, waiting for transfers between devices, shards(): lax.all_gather(front_z, 'row', axis=1, tiled=True)  27.1 us
    reduce_scatter x1, waiting for transfers between devices, shards(): lax.psum_scatter(out_part.astype(jnp.bfloat16), 'col', scatter_dimension=...  26.5 us
  transfers between devices with their start and end apart: 10, of which 10 were waited for; matrix products, arithmetic and copies ran while one was open for 0% of the time, Pallas kernels for 0%

profile of v1, /device:TPU:0, one launch (start us, length us, event | category | flops | bytes accessed | tf_op | source)
XLA Modules:
  0.0 439.8 jit_solution(17107274212358703769)
XLA Ops:
  7.2 0.7 all-gather.4.cloned.1.call-update
  8.0 32.3 %all-gather.4.cloned.1.call-done = bf16[2048,256]{0,1:T(8,128)(2,1)} async-done(((bf16[2048,64]{0,1:T(8,128)(2,1)}), bf16[2048,256]{0,1:T(8,128)(2,1)}) %all-gather.4.cloned.1.call-update) | async-done | bytes 1048592 | tf_op jit(solution)/shard_map/all_gather | solution.py:19
  40.3 7.3 %fusion.10 = f32[2048,256]{0,1:T(8,128)} fusion(bf16[2048,2048]{1,0:T(8,128)(2,1)} %param.8, bf16[2048,256]{0,1:T(8,128)(2,1)} %all-gather.4.cloned.1.call-done), kind=kOutput, calls=%fused_computation.19 | convolution fusion | flops 2147483648 | bytes 11534336 | tf_op jit(solution)/shard_map/dot_general | solution.py:17
  47.7 34.7 %reduce-scatter.5.cloned.1.call-done = f32[2048,64]{0,1:T(8,128)} async-done(((f32[2048,256]{0,1:T(8,128)}), f32[2048,64]{0,1:T(8,128)}) %reduce-scatter.5.cloned.1.call-update) | async-done | bytes 524304 | tf_op jit(solution)/shard_map/reduce_scatter | solution.py:22
  82.3 1.8 convert_element_type.53
  84.2 27.1 %all-gather.6.cloned.1.call-done = bf16[2048,256]{0,1:T(8,128)(2,1)} async-done(((bf16[2048,64]{0,1:T(8,128)(2,1)}), bf16[2048,256]{0,1:T(8,128)(2,1)}) %all-gather.6.cloned.1.call-update) | async-done | bytes 1048592 | tf_op jit(solution)/shard_map/all_gather | solution.py:25
  111.3 2.7 convolution_bitcast_fusion
  114.1 0.2 subtract_reduce_fusion
  114.3 21.7 %reduce-scatter.7.cloned.1.call-done = f32[128,256]{0,1:T(8,128)} async-done(((f32[512,256]{0,1:T(8,128)}), f32[128,256]{0,1:T(8,128)}) %reduce-scatter.7.cloned.1.call-update) | async-done | bytes 131088 | tf_op jit(solution)/shard_map/reduce_scatter | solution.py:26
  136.0 0.9 convert_element_type.56
  136.9 1.9 all_gather.17
  138.9 0.1 copy.10
  139.0 0.4 fusion.5
  139.5 0.1 copy.11
  139.6 0.1 fusion.4
  139.7 4.8 %fusion = bf16[4096,256]{0,1:T(8,128)(2,1)} fusion(bf16[512,256]{1,0:T(8,128)(2,1)S(1)} %fusion.4, bf16[4096,512]{1,0:T(8,128)(2,1)} %param.10), kind=kOutput, calls=%fused_computation.1 | convolution fusion | flops 1074790400 | bytes 6553600 | tf_op jit(solution)/shard_map/dot_general | solution.py:40
  144.5 84.5 %all-reduce.4.cloned.1.call-done = bf16[4096,256]{0,1:T(8,128)(2,1)} async-done(((bf16[4096,256]{0,1:T(8,128)(2,1)}), bf16[4096,256]{0,1:T(8,128)(2,1)}) %all-reduce.4.cloned.1.call-update) | async-done | bytes 2097168 | tf_op jit(solution)/shard_map/psum | solution.py:41
  229.1 71.4 %all-reduce.6.cloned.1.call-done = bf16[4096,256]{0,1:T(8,128)(2,1)} async-done(((bf16[4096,256]{0,1:T(8,128)(2,1)}), bf16[4096,256]{0,1:T(8,128)(2,1)}) %all-reduce.6.cloned.1.call-update) | async-done | bytes 2097168 | tf_op jit(solution)/shard_map/psum | solution.py:42
  300.6 4.8 %fusion.3 = bf16[512,256]{0,1:T(8,128)(2,1)} fusion(bf16[4096,256]{0,1:T(8,128)(2,1)} %all-reduce.6.cloned.1.call-done, bf16[4096,512]{1,0:T(8,128)(2,1)} %param.10), kind=kOutput, calls=%fused_computation.8 | convolution fusion | flops 1073872896 | bytes 6553600 | tf_op jit(solution)/shard_map/dot_general | solution.py:8
  305.4 0.6 dynamic_slice.10
  306.7 17.1 %all-reduce.8.cloned.1.call-done = bf16[512,256]{0,1:T(8,128)(2,1)} async-done(((bf16[512,256]{0,1:T(8,128)(2,1)}), bf16[512,256]{0,1:T(8,128)(2,1)}) %all-reduce.8.cloned.1.call-update) | async-done | bytes 262160 | tf_op jit(solution)/shard_map/psum | solution.py:43
  323.8 0.8 constant_dynamic-slice_fusion
  324.6 13.1 %all_gather.18 = bf16[512,256]{0,1:T(8,128)(2,1)S(1)} all-gather(bf16[128,256]{0,1:T(8,128)(2,1)S(1)} %constant_dynamic-slice_fusion), channel_id=1, replica_groups=mesh['leaf'=2,'row'=4,'col'=4] {'col'}, dimensions={0}, use_global_device_ids=true | all-gather | bytes 327680 | tf_op jit(solution)/shard_map/all_gather | solution.py:50
  337.7 1.7 fusion.2
  339.5 0.0 all-gather.8.cloned.1.call-start
  339.5 28.2 %reduce-scatter.9.cloned.1.call-done = bf16[2048,64]{0,1:T(8,128)(2,1)} async-done(((bf16[2048,256]{0,1:T(8,128)(2,1)}), bf16[2048,64]{0,1:T(8,128)(2,1)}) %reduce-scatter.9.cloned.1.call-update) | async-done | bytes 262160 | tf_op jit(solution)/shard_map/reduce_scatter | solution.py:53
  367.7 1.7 subtract_convert_fusion
  369.5 27.2 %all-gather.8.cloned.1.call-done = bf16[2048,256]{0,1:T(8,128)(2,1)} async-done(((bf16[2048,64]{0,1:T(8,128)(2,1)}), bf16[2048,256]{0,1:T(8,128)(2,1)}) %all-gather.8.cloned.1.call-update) | async-done | bytes 1048592 | tf_op jit(solution)/shard_map/all_gather | solution.py:57
  396.7 7.0 %fusion.1 = bf16[2048,256]{0,1:T(8,128)(2,1)} fusion(bf16[2048,256]{0,1:T(8,128)(2,1)} %all-gather.8.cloned.1.call-done, bf16[2048,2048]{1,0:T(8,128)(2,1)} %param.8), kind=kOutput, calls=%fused_computation.4 | convolution fusion | flops 2148007936 | bytes 10485760 | tf_op jit(solution)/shard_map/dot_general | solution.py:8
  403.7 0.9 copy.12
  404.7 26.5 %reduce-scatter.11.cloned.1.call-done = bf16[2048,64]{0,1:T(8,128)(2,1)} async-done(((bf16[2048,256]{0,1:T(8,128)(2,1)}), bf16[2048,64]{0,1:T(8,128)(2,1)}) %reduce-scatter.11.cloned.1.call-update) | async-done | bytes 262160 | tf_op jit(solution)/shard_map/reduce_scatter | solution.py:58
  431.2 1.8 convert_element_type.68
  (29 shorter events, 0.6 us)
Async XLA Ops:
  7.2 104.1 %copy-start = (bf16[2048,512]{1,0:T(8,128)(2,1)S(1)}, bf16[2048,512]{1,0:T(8,128)(2,1)}, u32[]{:S(2)}) copy-start(bf16[2048,512]{1,0:T(8,128)(2,1)} %param.9) | copy-start | bytes 6291460
  7.2 33.1 %all-gather.4.cloned.1.call-start = ((), (), s32[]{:S(2)}) async-start(), calls=%async_computation.4 | async-start | bytes 1310720 | tf_op jit(solution)/shard_map/all_gather | solution.py:19
  7.9 74.4 %reduce-scatter.5.cloned.1.call-start = ((), (), s32[]{:S(2)}) async-start(), calls=%async_computation.5 | async-start | bytes 2621440 | tf_op jit(solution)/shard_map/reduce_scatter | solution.py:22
  47.6 63.7 %all-gather.6.cloned.1.call-start = ((), (), s32[]{:S(2)}) async-start(), calls=%async_computation.6 | async-start | bytes 1310720 | tf_op jit(solution)/shard_map/all_gather | solution.py:25
  84.1 30.0 %copy-start.4 = (s32[2,16]{1,0:T(2,128)S(1)}, s32[2,16]{1,0:T(2,128)}, u32[]{:S(2)}) copy-start(s32[2,16]{1,0:T(2,128)} %param.11) | copy-start | bytes 388
  84.2 51.9 %reduce-scatter.7.cloned.1.call-start = ((), (), s32[]{:S(2)}) async-start(), calls=%async_computation.7 | async-start | bytes 655360 | tf_op jit(solution)/shard_map/reduce_scatter | solution.py:26
  114.0 25.5 %copy-start.3 = (bf16[512,256]{1,0:T(8,128)(2,1)S(1)}, bf16[512,256]{1,0:T(8,128)(2,1)}, u32[]{:S(2)}) copy-start(bf16[512,256]{1,0:T(8,128)(2,1)} %param.7) | copy-start | bytes 786436
  114.1 115.0 %all-reduce.4.cloned.1.call-start = ((), (), s32[]{:S(2)}) async-start(), calls=%async_computation.8 | async-start | bytes 4194304 | tf_op jit(solution)/shard_map/psum | solution.py:41
  144.5 156.1 %all-reduce.6.cloned.1.call-start = ((), (), s32[]{:S(2)}) async-start(), calls=%async_computation.9 | async-start | bytes 4194304 | tf_op jit(solution)/shard_map/psum | solution.py:42
  229.1 94.7 %all-reduce.8.cloned.1.call-start = ((), (), s32[]{:S(2)}) async-start(), calls=%async_computation.10 | async-start | bytes 524288 | tf_op jit(solution)/shard_map/psum | solution.py:43
  305.4 62.4 %reduce-scatter.9.cloned.1.call-start = ((), (), s32[]{:S(2)}) async-start(), calls=%async_computation.11 | async-start | bytes 1310720 | tf_op jit(solution)/shard_map/reduce_scatter | solution.py:53
  337.7 30.0 %copy-start.1 = (f32[2048,64]{0,1:T(8,128)S(1)}, f32[2048,64]{0,1:T(8,128)}, u32[]{:S(2)}) copy-start(f32[2048,64]{0,1:T(8,128)} %reduce-scatter.5.cloned.1.call-done) | copy-start | bytes 1572868
  339.5 57.2 %all-gather.8.cloned.1.call-start = ((), (), s32[]{:S(2)}) async-start(), calls=%async_computation.12 | async-start | bytes 1310720 | tf_op jit(solution)/shard_map/all_gather | solution.py:57
  369.5 34.3 %copy-start.2 = (bf16[512,256]{0,1:T(8,128)(2,1)S(1)}, bf16[512,256]{0,1:T(8,128)(2,1)}, u32[]{:S(2)}) copy-start(bf16[512,256]{0,1:T(8,128)(2,1)} %all-reduce.8.cloned.1.call-done) | copy-start | bytes 786436
  369.5 61.7 %reduce-scatter.11.cloned.1.call-start = ((), (), s32[]{:S(2)}) async-start(), calls=%async_computation.13 | async-start | bytes 1310720 | tf_op jit(solution)/shard_map/reduce_scatter | solution.py:58
Sparse Core Ops, SparseCore 0:
  9.6 30.6 all-gather.3
  47.7 34.5 reduce-scatter.4
  84.8 26.4 all-gather.5
  114.2 21.8 reduce-scatter.6
  144.6 84.3 all-reduce.3
  232.0 68.5 all-reduce.5
  305.5 18.2 all-reduce.7
  339.6 28.0 reduce-scatter.8
  370.2 26.4 all-gather.7
  403.9 27.2 reduce-scatter.10
